TPU v7x, 128 devices: a whole 4x4x4 slice. The times are simulated.
128 devices in a mesh: gx: 16 (over x, z), gy: 8 (over y, core).
Axes of the slice: x: 4, y: 4, z: 4, core: 2. Of those that a mesh axis runs over, the one named last changes fastest.
Arguments:
- old_states: float32 [32768, 12, 512], P(('gx', 'gy')), may hold values from -6 to 6
- new_place: int32 [32768], P(('gx', 'gy')), may hold values from -1 to 16383, as said below
- vectors_x: float32 [10, 10], replicated, may hold values from -2 to 2
- vectors_s: float32 [10, 10], replicated, may hold values from -2 to 2
- vectors_w: float32 [16, 10, 10], replicated, may hold values from -2 to 2
- values_x: float32 [10], replicated, may hold values from 0.2 to 5
- values_s: float32 [10], replicated, may hold values from 0.2 to 5
- values_w: float32 [16, 10], replicated, may hold values from 0.2 to 5
Outputs:
- new_states: float32 [64, 16, 16, 12, 512], P('gx', 'gy')
- correction: float32 [512, 128, 128], P('gx', 'gy')
Inputs may be any that keep to these rules, and one draw needn't show every extreme that they name: `new_place`: every element number appears in exactly one slot; the other slots hold -1. One device's slots send at most 2 elements to any one device, and some pairs reach 2; some devices have all 256 slots filled.
All inputs are finite; a program needn't handle non-finite values.
Results may differ from a plain program's by a relative error of at most 0.00007.
Values sent between devices are 32-bit elements; how exact they have to be, the bound alone decides.
A program may use at most 128 MiB of HBM per device.

v0:
```python
import functools
import jax
import jax.numpy as jnp
from jax import lax
from jax.experimental import pallas as pl
from jax.experimental.pallas import tpu as pltpu
from jax.sharding import PartitionSpec as P

MESH = pl.DeviceIdType.MESH
HIGHEST = lax.Precision.HIGHEST
F32 = jnp.float32

FIELDS = 12
FPC = 4
NCH = FIELDS // FPC
W = 4 * FPC
ROWS = 256
MB = 1024 * 1024


def send_order():
    left = [
        (a, b, c) for a in range(4) for b in range(4) for c in range(4) if (a, b, c) != (0, 0, 0)
    ]
    load = [0] * 6
    order = []

    def with_step(step):
        out = list(load)
        for axis, value in enumerate(step):
            if value in (1, 2):
                out[2 * axis] += 1
            if value in (2, 3):
                out[2 * axis + 1] += 1
        return out

    def cost(step):
        after = with_step(step)
        total = sum(after)
        return (6 * max(after) - total, sum(v * v for v in after) * 6 - total * total, step)

    while left:
        best = min(left, key=cost)
        left.remove(best)
        load[:] = with_step(best)
        order.append(best)
    return order


ORDER = send_order()


def my_place():
    gx = lax.axis_index("gx")
    gy = lax.axis_index("gy")
    return gx, gy


def peers():
    gx, gy = my_place()
    x, z = gx // 4, lax.rem(gx, 4)
    y, core = gy // 2, lax.rem(gy, 2)
    other = 1 - core
    out = [(gx, y * 2 + other)]
    for to_core in (core, other):
        for step in ORDER:
            hop = [step[i] * (1 - core) + (4 - step[i]) * core for i in range(3)]
            px = lax.rem(x + hop[0], 4)
            py = lax.rem(y + hop[1], 4)
            pz = lax.rem(z + hop[2], 4)
            out.append((px * 4 + pz, py * 2 + to_core))
    return out


def pack_kernel(place_ref, old_ref, out_ref, marks_ref, idx_v, idx_s, sem):
    @pl.when(pl.program_id(0) == 0)
    def _():
        place = place_ref[...]
        live = place >= 0
        p = jnp.maximum(place, 0)
        layer = p & 15
        es = (p >> 4) & 15
        ex = p >> 8
        target = ((ex >> 2) * 8 + (es >> 1)).astype(F32)
        row = (((ex & 3) * 2 + (es & 1)) * 16 + layer).astype(F32)
        key = jnp.where(live, target, -1.0)
        ri = lax.broadcasted_iota(jnp.int32, (ROWS, ROWS), 0)
        ci = lax.broadcasted_iota(jnp.int32, (ROWS, ROWS), 1)
        rf = ri.astype(F32)
        cf = ci.astype(F32)
        same = ri == ci
        key_b = jnp.broadcast_to(key, (ROWS, ROWS))
        key_c = jnp.sum(jnp.where(same, key_b, 0.0), axis=1, keepdims=True)
        rank = jnp.sum(
            jnp.where((key_c == key_b) & (ri < ci), 1.0, 0.0), axis=0, keepdims=True
        )
        pos = jnp.where(live, target * 2.0 + rank, -1.0)
        pos_b = jnp.broadcast_to(pos, (ROWS, ROWS))
        pos_c = jnp.sum(jnp.where(same, pos_b, 0.0), axis=1, keepdims=True)
        idx = jnp.sum(jnp.where(pos_c == cf, rf, 0.0), axis=0, keepdims=True)
        idx_v[...] = idx.astype(jnp.int32)
        row_b = jnp.broadcast_to(row + 1.0, (ROWS, ROWS))
        mark = jnp.sum(jnp.where(pos_b == rf, row_b, 0.0), axis=1, keepdims=True) - 1.0
        marks_ref[...] = jnp.broadcast_to(mark, (ROWS, 128))
        copy = pltpu.make_async_copy(idx_v, idx_s, sem)
        copy.start()
        copy.wait()

    def body(step, _):
        for more in range(4):
            r = step * 4 + more
            s = idx_s[0, r]
            base = (s >> 3) * 32 + (s & 7)
            for f in range(FPC):
                out_ref[0, r, 4 * f : 4 * f + 4, :] = old_ref[f, pl.ds(base, 4, stride=8), :]
        return 0

    lax.fori_loop(0, ROWS // 4, body, 0)


def pack(new_place, old_view):
    return pl.pallas_call(
        pack_kernel,
        grid=(NCH,),
        in_specs=[
            pl.BlockSpec((1, ROWS), lambda c: (0, 0)),
            pl.BlockSpec((FPC, ROWS * 4, 128), lambda c: (c, 0, 0)),
        ],
        out_specs=[
            pl.BlockSpec((1, ROWS, W, 128), lambda c: (c, 0, 0, 0)),
            pl.BlockSpec((ROWS, 128), lambda c: (0, 0)),
        ],
        out_shape=[
            jax.ShapeDtypeStruct((NCH, ROWS, W, 128), F32),
            jax.ShapeDtypeStruct((ROWS, 128), F32),
        ],
        scratch_shapes=[
            pltpu.VMEM((1, ROWS), jnp.int32),
            pltpu.SMEM((1, ROWS), jnp.int32),
            pltpu.SemaphoreType.DMA,
        ],
        name="pack",
    )(new_place, old_view)


def migrate_kernel(src, marks, dst, marks_out, ssem, rsem, msem_s, msem_r, lsem):
    gx, gy = my_place()
    me = gx * 8 + gy
    everyone = peers()
    barrier = pltpu.get_barrier_semaphore()

    def greet(k, _):
        d = lax.rem(me + k, 128)
        pl.semaphore_signal(
            barrier, inc=1, device_id=(d // 8, lax.rem(d, 8)), device_id_type=MESH
        )
        return 0

    lax.fori_loop(1, 128, greet, 0)
    own = []
    for ch in range(NCH):
        own.append(
            pltpu.make_async_copy(
                src.at[ch, pl.ds(2 * me, 2)], dst.at[ch, pl.ds(2 * me, 2)], lsem.at[ch]
            )
        )
    own.append(
        pltpu.make_async_copy(
            marks.at[pl.ds(2 * me, 2)], marks_out.at[pl.ds(2 * me, 2)], lsem.at[NCH]
        )
    )
    for copy in own:
        copy.start()
    pl.semaphore_wait(barrier, 127)
    for peer in everyone:
        d = peer[0] * 8 + peer[1]
        pltpu.make_async_remote_copy(
            marks.at[pl.ds(2 * d, 2)],
            marks_out.at[pl.ds(2 * me, 2)],
            msem_s,
            msem_r,
            device_id=peer,
            device_id_type=MESH,
        ).start()

    def chunk(ch, _):
        for peer in everyone:
            d = peer[0] * 8 + peer[1]
            pltpu.make_async_remote_copy(
                src.at[ch, pl.ds(2 * d, 2)],
                dst.at[ch, pl.ds(2 * me, 2)],
                ssem.at[ch],
                rsem.at[ch],
                device_id=peer,
                device_id_type=MESH,
            ).start()
        return 0

    lax.fori_loop(0, NCH, chunk, 0)
    some = pl.ds(0, ROWS - 2)
    pltpu.make_async_copy(marks.at[some], marks_out.at[some], msem_r).wait()
    pltpu.make_async_copy(marks.at[some], marks_out.at[some], msem_s).wait()
    for ch in range(NCH):
        pltpu.make_async_copy(src.at[ch, some], dst.at[ch, some], rsem.at[ch]).wait()
        pltpu.make_async_copy(src.at[ch, some], dst.at[ch, some], ssem.at[ch]).wait()
    for copy in own:
        copy.wait()


def migrate(packed, marks):
    marks = marks.reshape(ROWS, 1, 128)
    return pl.pallas_call(
        migrate_kernel,
        in_specs=[pl.BlockSpec(memory_space=pl.ANY)] * 2,
        out_specs=[pl.BlockSpec(memory_space=pl.ANY)] * 2,
        out_shape=[
            jax.ShapeDtypeStruct(packed.shape, F32),
            jax.ShapeDtypeStruct(marks.shape, F32),
        ],
        scratch_shapes=[
            pltpu.SemaphoreType.DMA((NCH,)),
            pltpu.SemaphoreType.DMA((NCH,)),
            pltpu.SemaphoreType.DMA,
            pltpu.SemaphoreType.DMA,
            pltpu.SemaphoreType.DMA((NCH + 1,)),
        ],
        compiler_params=pltpu.CompilerParams(collective_id=1, has_side_effects=True),
        name="migrate",
    )(packed, marks)


def unpack_kernel(marks_ref, recv_ref, out_ref, idx_v, idx_s, sem):
    @pl.when(pl.program_id(0) == 0)
    def _():
        rf = lax.broadcasted_iota(jnp.int32, (ROWS, 128), 0).astype(F32)
        nf = lax.broadcasted_iota(jnp.int32, (ROWS, 128), 1).astype(F32)
        idx = jnp.sum(jnp.where(marks_ref[...] == nf, rf, 0.0), axis=0, keepdims=True)
        idx_v[...] = idx.astype(jnp.int32)
        copy = pltpu.make_async_copy(idx_v, idx_s, sem)
        copy.start()
        copy.wait()

    def body(col, _):
        for layer in range(16):
            a = idx_s[0, col * 16 + layer]
            for f in range(FPC):
                start = (layer // 8) * 32 + layer % 8
                out_ref[col, f, pl.ds(start, 4, stride=8), :] = recv_ref[
                    0, a, 4 * f : 4 * f + 4, :
                ]
        return 0

    lax.fori_loop(0, 8, body, 0)


def unpack(marks, recv):
    return pl.pallas_call(
        unpack_kernel,
        grid=(NCH,),
        in_specs=[
            pl.BlockSpec((ROWS, 128), lambda c: (0, 0)),
            pl.BlockSpec((1, ROWS, W, 128), lambda c: (c, 0, 0, 0)),
        ],
        out_specs=pl.BlockSpec((8, FPC, 64, 128), lambda c: (0, c, 0, 0)),
        out_shape=jax.ShapeDtypeStruct((8, FIELDS, 64, 128), F32),
        scratch_shapes=[
            pltpu.VMEM((1, 128), jnp.int32),
            pltpu.SMEM((1, 128), jnp.int32),
            pltpu.SemaphoreType.DMA,
        ],
        name="unpack",
    )(marks, recv)


def lane_iota(rows):
    return lax.broadcasted_iota(jnp.int32, (rows, 128), 1)


def tile_of(k):
    return slice(k * 128, (k + 1) * 128)


def build_tables(vx, vs, vw, valx, vals, valw, pad, mat, mat_t, coef, wval, dcol):
    q = lax.broadcasted_iota(jnp.int32, (16, 128), 1)
    u_row = lax.broadcasted_iota(jnp.int32, (16, 128), 0)
    along = (q & 7) + 1
    u_of = jnp.where(q < 64, (q >> 3) + 1, jnp.where(q < 72, 0, jnp.where(q < 80, 9, along)))
    v_of = jnp.where(q < 80, along, jnp.where(q < 88, 0, 9))
    pick_u = jnp.where((u_row == u_of) & (q < 96), 1.0, 0.0)
    pick_v = jnp.where((u_row == v_of) & (q < 96), 1.0, 0.0)
    big_r = lax.broadcasted_iota(jnp.int32, (128, 128), 0)
    big_c = lax.broadcasted_iota(jnp.int32, (128, 128), 1)
    i_of = (big_r * 205) >> 11
    j_of = big_r - i_of * 10
    pick_i = jnp.where((big_c == i_of) & (big_r < 100), 1.0, 0.0)
    pick_j = jnp.where((big_c == j_of) & (big_r < 100), 1.0, 0.0)
    first = (((0,), (0,)), ((), ()))

    def padded(value, width=10):
        pad[...] = jnp.zeros((16, 128), F32)
        pad[0 : value.shape[0], 0:width] = value
        return pad[...]

    def grow(vec, pick_q, pick_row):
        side = lax.dot_general(
            padded(vec), pick_q, first, precision=HIGHEST, preferred_element_type=F32
        )
        return jnp.dot(pick_row, side, precision=HIGHEST, preferred_element_type=F32)

    both = grow(vx[...], pick_u, pick_i) * grow(vs[...], pick_v, pick_j)
    mat[...] = both
    mat_t[...] = both.T
    rows = padded(valx[...])[0:1, :]
    d = jnp.sum(pick_i * rows, axis=1, keepdims=True)
    rows = padded(vals[...])[0:1, :]
    d = d + jnp.sum(pick_j * rows, axis=1, keepdims=True)
    dcol[...] = jnp.broadcast_to(d, (128, 128))
    spread = jnp.where(u_row == (q & 15), 1.0, 0.0)
    for w in range(10):
        table = lax.dot_general(
            padded(vw[w]), spread, first, precision=HIGHEST, preferred_element_type=F32
        )
        for k in range(10):
            coef[w, k] = jnp.broadcast_to(table[k : k + 1, :], (8, 128))
    table = lax.dot_general(
        padded(valw[...]), spread, first, precision=HIGHEST, preferred_element_type=F32
    )
    for k in range(10):
        wval[k] = jnp.broadcast_to(table[k : k + 1, :], (8, 128))


def right_side(arrived, marks, points):
    nf = lane_iota(ROWS).astype(F32)
    chosen = jnp.where(marks == nf, 1.0, 0.0)
    for c in range(4):
        f0, f1, f2 = (arrived[pl.ds(4 * f + c, ROWS, stride=W), :] for f in range(3))
        rows = 3.0 * f0 - 3.0 * f1 + f2
        points[128 * c : 128 * (c + 1), :] = jnp.dot(
            rows.T, chosen, precision=HIGHEST, preferred_element_type=F32
        )


def gather_planes(points, planes):
    for i in range(8):
        planes[0, 8 * i : 8 * i + 8, :] = points[64 * i + 56 : 64 * i + 64, :]
        planes[1, 8 * i : 8 * i + 8, :] = points[64 * i : 64 * i + 8, :]


def neighbours():
    gx, gy = my_place()
    return (
        (lax.rem(gx + 1, 16), gy),
        (lax.rem(gx + 15, 16), gy),
        (gx, lax.rem(gy + 1, 8)),
        (gx, lax.rem(gy + 7, 8)),
    )


def plane_copies(sources, target, ssem, rsem, base):
    return [
        pltpu.make_async_remote_copy(
            sources[p],
            target.at[p],
            ssem.at[base + p],
            rsem.at[base + p],
            device_id=peer,
            device_id_type=MESH,
        )
        for p, peer in enumerate(neighbours())
    ]


def fill_inner(points, boxes):
    boxes[96:128, :] = jnp.zeros((32, 1280), F32)
    boxes[64:96, tile_of(0)] = jnp.zeros((32, 128), F32)
    boxes[64:96, tile_of(9)] = jnp.zeros((32, 128), F32)
    layer = lane_iota(64) & 15
    for k in range(8):
        value = points[pl.ds(k, 64, stride=8), :]
        boxes[0:64, tile_of(k + 1)] = value
        if k == 7:
            boxes[0:64, tile_of(0)] = jnp.where(layer == 0, 0.0, pltpu.roll(value, 1, 1))
        if k == 0:
            boxes[0:64, tile_of(9)] = jnp.where(layer == 15, 0.0, pltpu.roll(value, 127, 1))


def fill_faces(points, planes, arrived, boxes):
    lane = lane_iota(8)
    upper = (lane & 16) != 0
    for k in range(8):
        own = points[pl.ds(448 + k, 8, stride=8), :]
        far = arrived[0, pl.ds(k, 8, stride=8), :]
        boxes[64:72, tile_of(k + 1)] = pltpu.roll(jnp.where(lane >= 96, far, own), 32, 1)
        own = points[pl.ds(k, 8, stride=8), :]
        far = arrived[1, pl.ds(k, 8, stride=8), :]
        boxes[72:80, tile_of(k + 1)] = pltpu.roll(jnp.where(lane < 32, far, own), 96, 1)
        own = planes[0, pl.ds(k, 8, stride=8), :]
        far = arrived[2, pl.ds(k, 8, stride=8), :]
        boxes[80:88, tile_of(k + 1)] = jnp.where(
            upper, pltpu.roll(own, 16, 1), pltpu.roll(far, 112, 1)
        )
        own = planes[1, pl.ds(k, 8, stride=8), :]
        far = arrived[3, pl.ds(k, 8, stride=8), :]
        boxes[88:96, tile_of(k + 1)] = jnp.where(
            upper, pltpu.roll(far, 16, 1), pltpu.roll(own, 112, 1)
        )


def solve_boxes(boxes, half, mat, mat_t, coef, wval, dcol):
    half[0:104, :] = jnp.dot(
        mat[0:104, :], boxes[...], precision=HIGHEST, preferred_element_type=F32
    )
    half[104:128, :] = jnp.zeros((24, 1280), F32)

    def rows(t, _):
        at = pl.ds(pl.multiple_of(t * 8, 8), 8)
        section = [half[at, tile_of(w)] for w in range(10)]
        modal = []
        for k in range(10):
            total = coef[0, k] * section[0]
            for w in range(1, 10):
                total = total + coef[w, k] * section[w]
            modal.append(total / (dcol[at, :] + wval[k]))
        for w in range(10):
            total = coef[w, 0] * modal[0]
            for k in range(1, 10):
                total = total + coef[w, k] * modal[k]
            half[at, tile_of(w)] = total
        return 0

    lax.fori_loop(0, 13, rows, 0)
    boxes[0:96, :] = jnp.dot(
        mat_t[0:96, :], half[...], precision=HIGHEST, preferred_element_type=F32
    )


def return_planes(boxes, planes):
    for p, first in enumerate((72, 64, 88, 80)):
        for k in range(8):
            planes[p, pl.ds(k, 8, stride=8), :] = boxes[first : first + 8, tile_of(k + 1)]


def sum_cells(planes, arrived, boxes, sums, out):
    lane = lane_iota(8)
    upper = (lane & 16) != 0
    layer = lane_iota(64) & 15
    for k in range(8):
        value = boxes[0:64, tile_of(k + 1)]
        if k == 7:
            value = value + jnp.where(
                layer == 15, 0.0, pltpu.roll(boxes[0:64, tile_of(0)], 127, 1)
            )
        if k == 0:
            value = value + jnp.where(layer == 0, 0.0, pltpu.roll(boxes[0:64, tile_of(9)], 1, 1))
        sums[k] = value
        at = pl.ds(k, 8, stride=8)
        own, far = planes[0, at, :], arrived[0, at, :]
        sums[k, 0:8, :] += pltpu.roll(jnp.where(lane >= 96, far, own), 32, 1)
        own, far = planes[1, at, :], arrived[1, at, :]
        sums[k, 56:64, :] += pltpu.roll(jnp.where(lane < 32, far, own), 96, 1)
        own, far = planes[2, at, :], arrived[2, at, :]
        sums[k, pl.ds(0, 8, stride=8), :] += jnp.where(
            upper, pltpu.roll(own, 16, 1), pltpu.roll(far, 112, 1)
        )
        own, far = planes[3, at, :], arrived[3, at, :]
        sums[k, pl.ds(7, 8, stride=8), :] += jnp.where(
            upper, pltpu.roll(far, 16, 1), pltpu.roll(own, 112, 1)
        )
    src = lax.broadcasted_iota(jnp.int32, (128, 128), 0)
    to = lax.broadcasted_iota(jnp.int32, (128, 128), 1)
    order = jnp.where(to == (src & 15) * 8 + (src >> 4), 1.0, 0.0)
    group = lane_iota(64) >> 4
    for b in range(8):
        mixed = jnp.zeros((64, 128), F32)
        for k in range(8):
            turned = pltpu.roll(sums[k], ((k - b) % 8) * 16, 1) if k != b else sums[k]
            mixed = jnp.where(group == k, turned, mixed)
        mixed = jnp.dot(mixed, order, precision=HIGHEST, preferred_element_type=F32)
        for i in range(8):
            first = ((b // 2) * 8 + i) * 16 + (b % 2) * 8
            out[first : first + 8, :] = mixed[8 * i : 8 * i + 8, :]


def sweep_kernel(
    arrived, marks, vx, vs, vw, valx, vals, valw, out,
    pad, mat, mat_t, coef, wval, dcol, points, faces, faces_in, boxes, half,
    planes, planes_in, sums, ssem, rsem,
):
    barrier = pltpu.get_barrier_semaphore()
    for peer in neighbours():
        pl.semaphore_signal(barrier, inc=1, device_id=peer, device_id_type=MESH)
    build_tables(vx, vs, vw, valx, vals, valw, pad, mat, mat_t, coef, wval, dcol)
    right_side(arrived.at[0], marks[...], points)
    gather_planes(points, faces)
    pl.semaphore_wait(barrier, 4)
    sources = (points.at[pl.ds(448, 64)], points.at[pl.ds(0, 64)], faces.at[0], faces.at[1])
    copies = plane_copies(sources, faces_in, ssem, rsem, 0)
    for copy in copies:
        copy.start()
    fill_inner(points, boxes)
    for copy in copies:
        copy.wait()
    fill_faces(points, faces, faces_in, boxes)
    solve_boxes(boxes, half, mat, mat_t, coef, wval, dcol)
    return_planes(boxes, planes)
    copies = plane_copies([planes.at[p] for p in range(4)], planes_in, ssem, rsem, 4)
    for copy in copies:
        copy.start()
    for copy in copies:
        copy.wait()
    sum_cells(planes, planes_in, boxes, sums, out)


SWEEP_SCRATCH = [
    pltpu.VMEM((16, 128), F32),
    pltpu.VMEM((128, 128), F32),
    pltpu.VMEM((128, 128), F32),
    pltpu.VMEM((10, 10, 8, 128), F32),
    pltpu.VMEM((10, 8, 128), F32),
    pltpu.VMEM((128, 128), F32),
    pltpu.VMEM((512, 128), F32),
    pltpu.VMEM((2, 64, 128), F32),
    pltpu.VMEM((4, 64, 128), F32),
    pltpu.VMEM((128, 1280), F32),
    pltpu.VMEM((128, 1280), F32),
    pltpu.VMEM((4, 64, 128), F32),
    pltpu.VMEM((4, 64, 128), F32),
    pltpu.VMEM((8, 64, 128), F32),
    pltpu.SemaphoreType.DMA((8,)),
    pltpu.SemaphoreType.DMA((8,)),
]


def sweep(recv, marks, tables):
    whole = pl.BlockSpec(memory_space=pltpu.VMEM)
    return pl.pallas_call(
        sweep_kernel,
        grid=(1,),
        in_specs=[pl.BlockSpec((1, ROWS * W, 128), lambda c: (0, 0, 0))] + [whole] * 7,
        out_specs=whole,
        out_shape=jax.ShapeDtypeStruct((512, 128), F32),
        scratch_shapes=SWEEP_SCRATCH,
        compiler_params=pltpu.CompilerParams(collective_id=2, has_side_effects=True),
        name="sweep",
    )(recv, marks, *tables)


def shards(old_states, new_place, vectors_x, vectors_s, vectors_w, values_x, values_s, values_w):
    old_view = old_states.transpose(1, 0, 2).reshape(FIELDS, 32, 8, 4, 128)
    old_view = old_view.transpose(0, 1, 3, 2, 4).reshape(FIELDS, ROWS * 4, 128)
    packed, marks = pack(new_place.reshape(1, ROWS), old_view)
    recv, marks_in = migrate(packed, marks)
    marks_in = marks_in.reshape(ROWS, 128)
    tables = (
        vectors_x,
        vectors_s,
        vectors_w.transpose(1, 0, 2),
        values_x.reshape(1, 10),
        values_s.reshape(1, 10),
        values_w,
    )
    correction = sweep(recv.reshape(NCH, ROWS * W, 128), marks_in, tables)
    placed = unpack(marks_in, recv)
    placed = placed.reshape(4, 2, FIELDS, 2, 4, 8, 128).transpose(0, 1, 3, 5, 2, 4, 6)
    return placed.reshape(4, 2, 16, FIELDS, 512), correction.reshape(32, 16, 128)


def solution(mesh):
    placed = (P(("gx", "gy"), None, None), P(("gx", "gy")), P(), P(), P(), P(), P(), P())
    return jax.shard_map(
        shards,
        mesh=mesh,
        in_specs=placed,
        out_specs=(P("gx", "gy", None, None, None), P("gx", "gy", None)),
        check_vma=False,
    )
```

profile of v0, /device:TPU:1, one launch (start us, length us, event | category | flops | bytes accessed | tf_op | source)
XLA Modules:
  0.0 116.3 jit_solution(17330422822852917949)
XLA Ops:
  0.6 8.8 %pack.1 = (f32[3,256,16,128]{3,2,1,0:T(8,128)}, f32[256,128]{1,0:T(8,128)}) custom-call(s32[1,256]{1,0:T(1,128)} %bitcast.28, f32[12,1024,128]{2,1,0:T(8,128)} %bitcast.21), custom_call_target="tpu_custom_call" | custom-call | tf_op jit(solution)/shard_map/pack/pallas_call | solution.py:122
  9.4 83.9 %migrate.1 = (f32[3,256,16,128]{3,2,1,0:T(8,128)}, f32[256,1,128]{2,1,0:T(1,128)}) custom-call(f32[3,256,16,128]{3,2,1,0:T(8,128)} %get-tuple-element.6.src, f32[256,1,128]{2,1,0:T(1,128)} %bitcast.26), custom_call_target="tpu_custom_call" | custom-call | tf_op jit(solution)/shard_map/migrate/pallas_call | solution.py:212
  93.3 16.0 %sweep.1 = f32[512,128]{1,0:T(8,128)} custom-call(f32[3,4096,128]{2,1,0:T(8,128)} %bitcast.20, f32[256,128]{1,0:T(8,128)} %bitcast.24, f32[10,10]{1,0:T(8,128)} %vx.1, f32[10,10]{1,0:T(8,128)} %vs.1, f32[10,16,10]{2,1,0:T(8,128)} %bitcast.27, f32[1,10]{1,0:T(1,128)} %bitcast.29, f32[1,10]{1,0:T(1,128)} %bitcast.30, f32[16,10]{1,0:T(8,128)} %valw.1), custom_call_target="tpu_custom_call" | custom-call | tf_op jit(solution)/shard_map/sweep/pallas_call | solution.py:536
  109.3 0.0 copy-start
  109.3 6.2 %unpack.1 = f32[8,12,64,128]{3,2,1,0:T(8,128)} custom-call(f32[256,128]{1,0:T(8,128)} %bitcast.25, f32[3,256,16,128]{3,2,1,0:T(8,128)} %get-tuple-element.9.recv_ref), custom_call_target="tpu_custom_call" | custom-call | tf_op jit(solution)/shard_map/unpack/pallas_call | solution.py:257
  115.6 0.0 copy-done
  115.6 0.7 copy.11
Async XLA Ops:
  109.3 6.3 %copy-start = (f32[512,128]{1,0:T(8,128)S(1)}, f32[512,128]{1,0:T(8,128)}, u32[]{:S(2)}) copy-start(f32[512,128]{1,0:T(8,128)} %sweep.1) | copy-start | bytes 786436
where the time goes:
time: 118 us; the launch traced here: 116 us
  Pallas kernels  115 us (97%)
    pallas_call x1, Pallas kernels, migrate(): pl.pallas_call(migrate_kernel, in_specs=[pl.BlockSpec(memory_space=pl.ANY...  83.9 us
    pallas_call x1, Pallas kernels, sweep(): pl.pallas_call(sweep_kernel, grid=(1,), in_specs=[pl.BlockSpec((1, ROWS *...  16 us
    pallas_call x1, Pallas kernels, pack(): pl.pallas_call(pack_kernel, grid=(NCH,), in_specs=[pl.BlockSpec((1, ROWS)...  8.76 us
    pallas_call x1, Pallas kernels, unpack(): pl.pallas_call(unpack_kernel, grid=(NCH,), in_specs=[pl.BlockSpec((ROWS,...  6.25 us

commit v1 on v0

--- a/solution.py
+++ b/solution.py
@@ -11,11 +11,10 @@
 F32 = jnp.float32
 
 FIELDS = 12
-FPC = 4
+FPC = 2
 NCH = FIELDS // FPC
 W = 4 * FPC
 ROWS = 256
-MB = 1024 * 1024
 
 
 def send_order():
@@ -70,206 +69,6 @@
             pz = lax.rem(z + hop[2], 4)
             out.append((px * 4 + pz, py * 2 + to_core))
     return out
-
-
-def pack_kernel(place_ref, old_ref, out_ref, marks_ref, idx_v, idx_s, sem):
-    @pl.when(pl.program_id(0) == 0)
-    def _():
-        place = place_ref[...]
-        live = place >= 0
-        p = jnp.maximum(place, 0)
-        layer = p & 15
-        es = (p >> 4) & 15
-        ex = p >> 8
-        target = ((ex >> 2) * 8 + (es >> 1)).astype(F32)
-        row = (((ex & 3) * 2 + (es & 1)) * 16 + layer).astype(F32)
-        key = jnp.where(live, target, -1.0)
-        ri = lax.broadcasted_iota(jnp.int32, (ROWS, ROWS), 0)
-        ci = lax.broadcasted_iota(jnp.int32, (ROWS, ROWS), 1)
-        rf = ri.astype(F32)
-        cf = ci.astype(F32)
-        same = ri == ci
-        key_b = jnp.broadcast_to(key, (ROWS, ROWS))
-        key_c = jnp.sum(jnp.where(same, key_b, 0.0), axis=1, keepdims=True)
-        rank = jnp.sum(
-            jnp.where((key_c == key_b) & (ri < ci), 1.0, 0.0), axis=0, keepdims=True
-        )
-        pos = jnp.where(live, target * 2.0 + rank, -1.0)
-        pos_b = jnp.broadcast_to(pos, (ROWS, ROWS))
-        pos_c = jnp.sum(jnp.where(same, pos_b, 0.0), axis=1, keepdims=True)
-        idx = jnp.sum(jnp.where(pos_c == cf, rf, 0.0), axis=0, keepdims=True)
-        idx_v[...] = idx.astype(jnp.int32)
-        row_b = jnp.broadcast_to(row + 1.0, (ROWS, ROWS))
-        mark = jnp.sum(jnp.where(pos_b == rf, row_b, 0.0), axis=1, keepdims=True) - 1.0
-        marks_ref[...] = jnp.broadcast_to(mark, (ROWS, 128))
-        copy = pltpu.make_async_copy(idx_v, idx_s, sem)
-        copy.start()
-        copy.wait()
-
-    def body(step, _):
-        for more in range(4):
-            r = step * 4 + more
-            s = idx_s[0, r]
-            base = (s >> 3) * 32 + (s & 7)
-            for f in range(FPC):
-                out_ref[0, r, 4 * f : 4 * f + 4, :] = old_ref[f, pl.ds(base, 4, stride=8), :]
-        return 0
-
-    lax.fori_loop(0, ROWS // 4, body, 0)
-
-
-def pack(new_place, old_view):
-    return pl.pallas_call(
-        pack_kernel,
-        grid=(NCH,),
-        in_specs=[
-            pl.BlockSpec((1, ROWS), lambda c: (0, 0)),
-            pl.BlockSpec((FPC, ROWS * 4, 128), lambda c: (c, 0, 0)),
-        ],
-        out_specs=[
-            pl.BlockSpec((1, ROWS, W, 128), lambda c: (c, 0, 0, 0)),
-            pl.BlockSpec((ROWS, 128), lambda c: (0, 0)),
-        ],
-        out_shape=[
-            jax.ShapeDtypeStruct((NCH, ROWS, W, 128), F32),
-            jax.ShapeDtypeStruct((ROWS, 128), F32),
-        ],
-        scratch_shapes=[
-            pltpu.VMEM((1, ROWS), jnp.int32),
-            pltpu.SMEM((1, ROWS), jnp.int32),
-            pltpu.SemaphoreType.DMA,
-        ],
-        name="pack",
-    )(new_place, old_view)
-
-
-def migrate_kernel(src, marks, dst, marks_out, ssem, rsem, msem_s, msem_r, lsem):
-    gx, gy = my_place()
-    me = gx * 8 + gy
-    everyone = peers()
-    barrier = pltpu.get_barrier_semaphore()
-
-    def greet(k, _):
-        d = lax.rem(me + k, 128)
-        pl.semaphore_signal(
-            barrier, inc=1, device_id=(d // 8, lax.rem(d, 8)), device_id_type=MESH
-        )
-        return 0
-
-    lax.fori_loop(1, 128, greet, 0)
-    own = []
-    for ch in range(NCH):
-        own.append(
-            pltpu.make_async_copy(
-                src.at[ch, pl.ds(2 * me, 2)], dst.at[ch, pl.ds(2 * me, 2)], lsem.at[ch]
-            )
-        )
-    own.append(
-        pltpu.make_async_copy(
-            marks.at[pl.ds(2 * me, 2)], marks_out.at[pl.ds(2 * me, 2)], lsem.at[NCH]
-        )
-    )
-    for copy in own:
-        copy.start()
-    pl.semaphore_wait(barrier, 127)
-    for peer in everyone:
-        d = peer[0] * 8 + peer[1]
-        pltpu.make_async_remote_copy(
-            marks.at[pl.ds(2 * d, 2)],
-            marks_out.at[pl.ds(2 * me, 2)],
-            msem_s,
-            msem_r,
-            device_id=peer,
-            device_id_type=MESH,
-        ).start()
-
-    def chunk(ch, _):
-        for peer in everyone:
-            d = peer[0] * 8 + peer[1]
-            pltpu.make_async_remote_copy(
-                src.at[ch, pl.ds(2 * d, 2)],
-                dst.at[ch, pl.ds(2 * me, 2)],
-                ssem.at[ch],
-                rsem.at[ch],
-                device_id=peer,
-                device_id_type=MESH,
-            ).start()
-        return 0
-
-    lax.fori_loop(0, NCH, chunk, 0)
-    some = pl.ds(0, ROWS - 2)
-    pltpu.make_async_copy(marks.at[some], marks_out.at[some], msem_r).wait()
-    pltpu.make_async_copy(marks.at[some], marks_out.at[some], msem_s).wait()
-    for ch in range(NCH):
-        pltpu.make_async_copy(src.at[ch, some], dst.at[ch, some], rsem.at[ch]).wait()
-        pltpu.make_async_copy(src.at[ch, some], dst.at[ch, some], ssem.at[ch]).wait()
-    for copy in own:
-        copy.wait()
-
-
-def migrate(packed, marks):
-    marks = marks.reshape(ROWS, 1, 128)
-    return pl.pallas_call(
-        migrate_kernel,
-        in_specs=[pl.BlockSpec(memory_space=pl.ANY)] * 2,
-        out_specs=[pl.BlockSpec(memory_space=pl.ANY)] * 2,
-        out_shape=[
-            jax.ShapeDtypeStruct(packed.shape, F32),
-            jax.ShapeDtypeStruct(marks.shape, F32),
-        ],
-        scratch_shapes=[
-            pltpu.SemaphoreType.DMA((NCH,)),
-            pltpu.SemaphoreType.DMA((NCH,)),
-            pltpu.SemaphoreType.DMA,
-            pltpu.SemaphoreType.DMA,
-            pltpu.SemaphoreType.DMA((NCH + 1,)),
-        ],
-        compiler_params=pltpu.CompilerParams(collective_id=1, has_side_effects=True),
-        name="migrate",
-    )(packed, marks)
-
-
-def unpack_kernel(marks_ref, recv_ref, out_ref, idx_v, idx_s, sem):
-    @pl.when(pl.program_id(0) == 0)
-    def _():
-        rf = lax.broadcasted_iota(jnp.int32, (ROWS, 128), 0).astype(F32)
-        nf = lax.broadcasted_iota(jnp.int32, (ROWS, 128), 1).astype(F32)
-        idx = jnp.sum(jnp.where(marks_ref[...] == nf, rf, 0.0), axis=0, keepdims=True)
-        idx_v[...] = idx.astype(jnp.int32)
-        copy = pltpu.make_async_copy(idx_v, idx_s, sem)
-        copy.start()
-        copy.wait()
-
-    def body(col, _):
-        for layer in range(16):
-            a = idx_s[0, col * 16 + layer]
-            for f in range(FPC):
-                start = (layer // 8) * 32 + layer % 8
-                out_ref[col, f, pl.ds(start, 4, stride=8), :] = recv_ref[
-                    0, a, 4 * f : 4 * f + 4, :
-                ]
-        return 0
-
-    lax.fori_loop(0, 8, body, 0)
-
-
-def unpack(marks, recv):
-    return pl.pallas_call(
-        unpack_kernel,
-        grid=(NCH,),
-        in_specs=[
-            pl.BlockSpec((ROWS, 128), lambda c: (0, 0)),
-            pl.BlockSpec((1, ROWS, W, 128), lambda c: (c, 0, 0, 0)),
-        ],
-        out_specs=pl.BlockSpec((8, FPC, 64, 128), lambda c: (0, c, 0, 0)),
-        out_shape=jax.ShapeDtypeStruct((8, FIELDS, 64, 128), F32),
-        scratch_shapes=[
-            pltpu.VMEM((1, 128), jnp.int32),
-            pltpu.SMEM((1, 128), jnp.int32),
-            pltpu.SemaphoreType.DMA,
-        ],
-        name="unpack",
-    )(marks, recv)
 
 
 def lane_iota(rows):
@@ -333,7 +132,9 @@
     nf = lane_iota(ROWS).astype(F32)
     chosen = jnp.where(marks == nf, 1.0, 0.0)
     for c in range(4):
-        f0, f1, f2 = (arrived[pl.ds(4 * f + c, ROWS, stride=W), :] for f in range(3))
+        f0, f1, f2 = (
+            arrived[f // FPC][pl.ds(4 * (f % FPC) + c, ROWS, stride=W), :] for f in range(3)
+        )
         rows = 3.0 * f0 - 3.0 * f1 + f2
         points[128 * c : 128 * (c + 1), :] = jnp.dot(
             rows.T, chosen, precision=HIGHEST, preferred_element_type=F32
@@ -481,37 +282,207 @@
             out[first : first + 8, :] = mixed[8 * i : 8 * i + 8, :]
 
 
-def sweep_kernel(
-    arrived, marks, vx, vs, vw, valx, vals, valw, out,
-    pad, mat, mat_t, coef, wval, dcol, points, faces, faces_in, boxes, half,
-    planes, planes_in, sums, ssem, rsem,
-):
+def target_rows(place, idx_v, marks):
+    live = place >= 0
+    p = jnp.maximum(place, 0)
+    layer = p & 15
+    es = (p >> 4) & 15
+    ex = p >> 8
+    target = ((ex >> 2) * 8 + (es >> 1)).astype(F32)
+    row = (((ex & 3) * 2 + (es & 1)) * 16 + layer).astype(F32)
+    key = jnp.where(live, target, -1.0)
+    ri = lax.broadcasted_iota(jnp.int32, (ROWS, ROWS), 0)
+    ci = lax.broadcasted_iota(jnp.int32, (ROWS, ROWS), 1)
+    rf = ri.astype(F32)
+    cf = ci.astype(F32)
+    same = ri == ci
+    key_b = jnp.broadcast_to(key, (ROWS, ROWS))
+    key_c = jnp.sum(jnp.where(same, key_b, 0.0), axis=1, keepdims=True)
+    rank = jnp.sum(jnp.where((key_c == key_b) & (ri < ci), 1.0, 0.0), axis=0, keepdims=True)
+    pos = jnp.where(live, target * 2.0 + rank, -1.0)
+    pos_b = jnp.broadcast_to(pos, (ROWS, ROWS))
+    pos_c = jnp.sum(jnp.where(same, pos_b, 0.0), axis=1, keepdims=True)
+    idx = jnp.sum(jnp.where(pos_c == cf, rf, 0.0), axis=0, keepdims=True)
+    idx_v[...] = idx.astype(jnp.int32)
+    row_b = jnp.broadcast_to(row + 1.0, (ROWS, ROWS))
+    mark = jnp.sum(jnp.where(pos_b == rf, row_b, 0.0), axis=1, keepdims=True) - 1.0
+    marks[...] = jnp.broadcast_to(mark, (ROWS, 128)).reshape(ROWS, 1, 128)
+
+
+def pack_chunk(idx_s, old, packed):
+    def body(step, _):
+        for more in range(4):
+            r = step * 4 + more
+            s = idx_s[0, r] & (ROWS - 1)
+            base = (s >> 3) * 32 + (s & 7)
+            for f in range(FPC):
+                packed[r, 4 * f : 4 * f + 4, :] = old[f, pl.ds(base, 4, stride=8), :]
+        return 0
+
+    lax.fori_loop(0, ROWS // 4, body, 0)
+
+
+def arrived_rows(marks, idx_v):
+    rf = lax.broadcasted_iota(jnp.int32, (ROWS, 128), 0).astype(F32)
+    nf = lane_iota(ROWS).astype(F32)
+    idx = jnp.sum(jnp.where(marks == nf, rf, 0.0), axis=0, keepdims=True)
+    idx_v[...] = idx.astype(jnp.int32)
+
+
+def unpack_chunk(idx_s, recv, stage):
+    def body(col, _):
+        for layer in range(16):
+            a = idx_s[0, col * 16 + layer] & (ROWS - 1)
+            start = (layer // 8) * 32 + layer % 8
+            for f in range(FPC):
+                stage[col, f, pl.ds(start, 4, stride=8), :] = recv[a, 4 * f : 4 * f + 4, :]
+        return 0
+
+    lax.fori_loop(0, 8, body, 0)
+
+
+def whole_kernel(place, old, vx, vs, vw, valx, vals, valw, placed, out, scratch):
+    (
+        idx_v, idx_s, pos_v, pos_s, marks, marks_in, olds, packs, recvs, stages,
+        pad, mat, mat_t, coef, wval, dcol, points, faces, faces_in, boxes, half,
+        planes, planes_in, sums, ssem, rsem, msem, hssem, hrsem, osem, wsem, lsem, isem,
+    ) = scratch
+    gx, gy = my_place()
+    me = gx * 8 + gy
+    everyone = peers()
     barrier = pltpu.get_barrier_semaphore()
-    for peer in neighbours():
-        pl.semaphore_signal(barrier, inc=1, device_id=peer, device_id_type=MESH)
+    loads = [
+        pltpu.make_async_copy(old.at[pl.ds(FPC * ch, FPC)], olds[ch], osem.at[ch])
+        for ch in range(NCH)
+    ]
+    for copy in loads:
+        copy.start()
+
+    def greet(k, _):
+        d = lax.rem(me + k, 128)
+        pl.semaphore_signal(
+            barrier, inc=1, device_id=(d // 8, lax.rem(d, 8)), device_id_type=MESH
+        )
+        return 0
+
+    lax.fori_loop(1, 128, greet, 0)
+    target_rows(place[...], idx_v, marks)
+    copy = pltpu.make_async_copy(idx_v, idx_s, isem.at[0])
+    copy.start()
+    copy.wait()
+    own = []
+
+    def pack(ch):
+        loads[ch].wait()
+        pack_chunk(idx_s, olds[ch], packs[ch])
+
+    def send_one(source, target, send_sem, recv_sem, peer):
+        d = peer[0] * 8 + peer[1]
+        pltpu.make_async_remote_copy(
+            source.at[pl.ds(2 * d, 2)],
+            target.at[pl.ds(2 * me, 2)],
+            send_sem,
+            recv_sem,
+            device_id=peer,
+            device_id_type=MESH,
+        ).start()
+
+    def keep_own(source, target, sem):
+        copy = pltpu.make_async_copy(
+            source.at[pl.ds(2 * me, 2)], target.at[pl.ds(2 * me, 2)], sem
+        )
+        copy.start()
+        own.append(copy)
+
+    def send(ch):
+        for peer in everyone:
+            send_one(packs[ch], recvs[ch], ssem.at[ch], rsem.at[ch], peer)
+        keep_own(packs[ch], recvs[ch], lsem.at[ch])
+
+    some = pl.ds(0, ROWS - 2)
+
+    def arrive(ch):
+        pltpu.make_async_copy(packs[ch].at[some], recvs[ch].at[some], rsem.at[ch]).wait()
+        own[ch].wait()
+
+    def unpack(ch):
+        unpack_chunk(pos_s, recvs[ch], stages[ch])
+        copy = pltpu.make_async_copy(
+            stages[ch], placed.at[:, pl.ds(FPC * ch, FPC)], wsem.at[ch]
+        )
+        copy.start()
+        writes.append(copy)
+
+    writes = []
+    pack(0)
+    pl.semaphore_wait(barrier, 127)
+    send(0)
+    for peer in everyone:
+        send_one(marks, marks_in, msem.at[0], msem.at[1], peer)
+    pack(1)
+    send(1)
+    keep_own(marks, marks_in, lsem.at[NCH])
+    pack(2)
+    own_marks = own.pop()
+    send(2)
+    for ch in range(3, NCH):
+        pack(ch)
     build_tables(vx, vs, vw, valx, vals, valw, pad, mat, mat_t, coef, wval, dcol)
-    right_side(arrived.at[0], marks[...], points)
+    pltpu.make_async_copy(marks.at[some], marks_in.at[some], msem.at[1]).wait()
+    own_marks.wait()
+    marks_here = marks_in[...].reshape(ROWS, 128)
+    arrived_rows(marks_here, pos_v)
+    copy = pltpu.make_async_copy(pos_v, pos_s, isem.at[1])
+    copy.start()
+    copy.wait()
+    arrive(0)
+    arrive(1)
+    right_side([recvs[ch].reshape(ROWS * W, 128) for ch in range(2)], marks_here, points)
     gather_planes(points, faces)
-    pl.semaphore_wait(barrier, 4)
     sources = (points.at[pl.ds(448, 64)], points.at[pl.ds(0, 64)], faces.at[0], faces.at[1])
-    copies = plane_copies(sources, faces_in, ssem, rsem, 0)
-    for copy in copies:
+    halo = plane_copies(sources, faces_in, hssem, hrsem, 0)
+    for copy in halo:
         copy.start()
+    send(3)
     fill_inner(points, boxes)
-    for copy in copies:
+    unpack(0)
+    unpack(1)
+    for copy in halo:
         copy.wait()
     fill_faces(points, faces, faces_in, boxes)
     solve_boxes(boxes, half, mat, mat_t, coef, wval, dcol)
     return_planes(boxes, planes)
-    copies = plane_copies([planes.at[p] for p in range(4)], planes_in, ssem, rsem, 4)
-    for copy in copies:
+    halo = plane_copies([planes.at[p] for p in range(4)], planes_in, hssem, hrsem, 4)
+    for copy in halo:
         copy.start()
-    for copy in copies:
+    send(4)
+    send(5)
+    arrive(2)
+    unpack(2)
+    for copy in halo:
         copy.wait()
     sum_cells(planes, planes_in, boxes, sums, out)
-
-
-SWEEP_SCRATCH = [
+    for ch in range(3, NCH):
+        arrive(ch)
+        unpack(ch)
+    pltpu.make_async_copy(marks.at[some], marks_in.at[some], msem.at[0]).wait()
+    for ch in range(NCH):
+        pltpu.make_async_copy(packs[ch].at[some], recvs[ch].at[some], ssem.at[ch]).wait()
+    for copy in writes:
+        copy.wait()
+
+
+SCRATCH = (
+    pltpu.VMEM((1, ROWS), jnp.int32),
+    pltpu.SMEM((1, ROWS), jnp.int32),
+    pltpu.VMEM((1, 128), jnp.int32),
+    pltpu.SMEM((1, 128), jnp.int32),
+    pltpu.VMEM((ROWS, 1, 128), F32),
+    pltpu.VMEM((ROWS, 1, 128), F32),
+    [pltpu.VMEM((FPC, ROWS * 4, 128), F32)] * NCH,
+    [pltpu.VMEM((ROWS, W, 128), F32)] * NCH,
+    [pltpu.VMEM((ROWS, W, 128), F32)] * NCH,
+    [pltpu.VMEM((8, FPC, 64, 128), F32)] * NCH,
     pltpu.VMEM((16, 128), F32),
     pltpu.VMEM((128, 128), F32),
     pltpu.VMEM((128, 128), F32),
@@ -526,32 +497,37 @@
     pltpu.VMEM((4, 64, 128), F32),
     pltpu.VMEM((4, 64, 128), F32),
     pltpu.VMEM((8, 64, 128), F32),
+    pltpu.SemaphoreType.DMA((NCH,)),
+    pltpu.SemaphoreType.DMA((NCH,)),
+    pltpu.SemaphoreType.DMA((2,)),
     pltpu.SemaphoreType.DMA((8,)),
     pltpu.SemaphoreType.DMA((8,)),
-]
-
-
-def sweep(recv, marks, tables):
-    whole = pl.BlockSpec(memory_space=pltpu.VMEM)
-    return pl.pallas_call(
-        sweep_kernel,
-        grid=(1,),
-        in_specs=[pl.BlockSpec((1, ROWS * W, 128), lambda c: (0, 0, 0))] + [whole] * 7,
-        out_specs=whole,
-        out_shape=jax.ShapeDtypeStruct((512, 128), F32),
-        scratch_shapes=SWEEP_SCRATCH,
-        compiler_params=pltpu.CompilerParams(collective_id=2, has_side_effects=True),
-        name="sweep",
-    )(recv, marks, *tables)
+    pltpu.SemaphoreType.DMA((NCH,)),
+    pltpu.SemaphoreType.DMA((NCH,)),
+    pltpu.SemaphoreType.DMA((NCH + 1,)),
+    pltpu.SemaphoreType.DMA((2,)),
+)
 
 
 def shards(old_states, new_place, vectors_x, vectors_s, vectors_w, values_x, values_s, values_w):
     old_view = old_states.transpose(1, 0, 2).reshape(FIELDS, 32, 8, 4, 128)
     old_view = old_view.transpose(0, 1, 3, 2, 4).reshape(FIELDS, ROWS * 4, 128)
-    packed, marks = pack(new_place.reshape(1, ROWS), old_view)
-    recv, marks_in = migrate(packed, marks)
-    marks_in = marks_in.reshape(ROWS, 128)
-    tables = (
+    vmem = pl.BlockSpec(memory_space=pltpu.VMEM)
+    far = pl.BlockSpec(memory_space=pl.ANY)
+    placed, correction = pl.pallas_call(
+        whole_kernel,
+        in_specs=[vmem, far] + [vmem] * 6,
+        out_specs=[far, vmem],
+        out_shape=[
+            jax.ShapeDtypeStruct((8, FIELDS, 64, 128), F32),
+            jax.ShapeDtypeStruct((512, 128), F32),
+        ],
+        scratch_shapes=[SCRATCH],
+        compiler_params=pltpu.CompilerParams(collective_id=1, has_side_effects=True),
+        name="migrate_and_sweep",
+    )(
+        new_place.reshape(1, ROWS),
+        old_view,
         vectors_x,
         vectors_s,
         vectors_w.transpose(1, 0, 2),
@@ -559,8 +535,6 @@
         values_s.reshape(1, 10),
         values_w,
     )
-    correction = sweep(recv.reshape(NCH, ROWS * W, 128), marks_in, tables)
-    placed = unpack(marks_in, recv)
     placed = placed.reshape(4, 2, FIELDS, 2, 4, 8, 128).transpose(0, 1, 3, 5, 2, 4, 6)
     return placed.reshape(4, 2, 16, FIELDS, 512), correction.reshape(32, 16, 128)
 

time: 118 us -> 93.1 us (0.79); the launches traced: 116 us -> 92.9 us
  Pallas kernels: 115 us -> 87.4 us
  local copies, waits for them, and re-layouts: 0.71 us -> 4.88 us
    pallas_call x4 -> x1, Pallas kernels: 115 us -> 87.4 us  [shards(): pl.pallas_call(whole_kernel, in_specs=[vmem, far] + [vmem] * 6, out_specs...]
    unnamed x3 -> x4, local copies, waits for them, and re-layouts: 0.71 us -> 4.88 us
where the time goes in v1:
time: 93.1 us; the launch traced here: 92.9 us
  Pallas kernels  87.4 us (94%)
  local copies, waits for them, and re-layouts  4.88 us (5%)
    pallas_call x1, Pallas kernels, shards(): pl.pallas_call(whole_kernel, in_specs=[vmem, far] + [vmem] * 6, out_specs...  87.4 us
    unnamed x4, local copies, waits for them, and re-layouts  4.88 us

profile of v1, /device:TPU:1, one launch (start us, length us, event | category | flops | bytes accessed | tf_op | source)
XLA Modules:
  0.0 92.9 jit_solution(2062808323462641158)
XLA Ops:
  0.6 87.4 %migrate_and_sweep.1 = (f32[8,12,64,128]{3,2,1,0:T(8,128)}, f32[512,128]{1,0:T(8,128)}) custom-call(s32[1,256]{1,0:T(1,128)} %bitcast.21, f32[12,1024,128]{2,1,0:T(8,128)} %bitcast.17, f32[10,10]{1,0:T(8,128)} %vx.1, f32[10,10]{1,0:T(8,128)} %vs.1, f32[10,16,10]{2,1,0:T(8,128)} %bitcast.20, f32[1,10]{1,0:T(1,128)} %bitcast.22, f32[1,10]{1,0:T(1,128)} %bitcast.23, ...), custom_call_target="tpu_custom_call" | custom-call | tf_op jit(solution)/shard_map/migrate_and_sweep/pallas_call | solution.py:517
  88.0 0.0 copy-start
  88.1 4.2 %copy.12 = f32[4,2,16,12,512]{4,2,3,1,0:T(8,128)} copy(f32[4,2,16,12,512]{4,2,3,1,0:T(8,128)} %bitcast.18) | data formatting | bytes 6291456
  92.2 0.0 copy-done
  92.2 0.7 copy.13
Async XLA Ops:
  88.0 4.2 %copy-start = (f32[512,128]{1,0:T(8,128)S(1)}, f32[512,128]{1,0:T(8,128)}, u32[]{:S(2)}) copy-start(f32[512,128]{1,0:T(8,128)} %get-tuple-element.5) | copy-start | bytes 786436

commit v2 on v1

--- a/solution.py
+++ b/solution.py
@@ -47,6 +47,7 @@
 
 
 ORDER = send_order()
+LAST = sorted(ORDER, key=lambda step: -sum(min(v, 4 - v) for v in step))
 
 
 def my_place():
@@ -55,14 +56,17 @@
     return gx, gy
 
 
-def peers():
+def peers(steps):
     gx, gy = my_place()
     x, z = gx // 4, lax.rem(gx, 4)
     y, core = gy // 2, lax.rem(gy, 2)
     other = 1 - core
     out = [(gx, y * 2 + other)]
-    for to_core in (core, other):
-        for step in ORDER:
+    pairs = [(to, step) for to in (core, other) for step in steps]
+    if steps is LAST:
+        pairs = [(to, step) for step in steps for to in (core, other)]
+    for to_core, step in pairs:
+        if True:
             hop = [step[i] * (1 - core) + (4 - step[i]) * core for i in range(3)]
             px = lax.rem(x + hop[0], 4)
             py = lax.rem(y + hop[1], 4)
@@ -329,13 +333,15 @@
     idx_v[...] = idx.astype(jnp.int32)
 
 
-def unpack_chunk(idx_s, recv, stage):
+def unpack_chunk(idx_s, recv, placed, first):
     def body(col, _):
         for layer in range(16):
             a = idx_s[0, col * 16 + layer] & (ROWS - 1)
             start = (layer // 8) * 32 + layer % 8
             for f in range(FPC):
-                stage[col, f, pl.ds(start, 4, stride=8), :] = recv[a, 4 * f : 4 * f + 4, :]
+                placed[col, first + f, pl.ds(start, 4, stride=8), :] = recv[
+                    a, 4 * f : 4 * f + 4, :
+                ]
         return 0
 
     lax.fori_loop(0, 8, body, 0)
@@ -343,13 +349,15 @@
 
 def whole_kernel(place, old, vx, vs, vw, valx, vals, valw, placed, out, scratch):
     (
-        idx_v, idx_s, pos_v, pos_s, marks, marks_in, olds, packs, recvs, stages,
+        idx_v, idx_s, pos_v, pos_s, marks, marks_in, olds, packs, recvs,
         pad, mat, mat_t, coef, wval, dcol, points, faces, faces_in, boxes, half,
-        planes, planes_in, sums, ssem, rsem, msem, hssem, hrsem, osem, wsem, lsem, isem,
+        planes, planes_in, sums, ssem, rsem, msem, hssem, hrsem, osem, lsem, isem,
     ) = scratch
     gx, gy = my_place()
     me = gx * 8 + gy
-    everyone = peers()
+    everyone = peers(ORDER)
+    last = peers(LAST)
+    last = last[1:] + last[:1]
     barrier = pltpu.get_barrier_semaphore()
     loads = [
         pltpu.make_async_copy(old.at[pl.ds(FPC * ch, FPC)], olds[ch], osem.at[ch])
@@ -395,7 +403,7 @@
         own.append(copy)
 
     def send(ch):
-        for peer in everyone:
+        for peer in everyone if ch < NCH - 1 else last:
             send_one(packs[ch], recvs[ch], ssem.at[ch], rsem.at[ch], peer)
         keep_own(packs[ch], recvs[ch], lsem.at[ch])
 
@@ -406,14 +414,8 @@
         own[ch].wait()
 
     def unpack(ch):
-        unpack_chunk(pos_s, recvs[ch], stages[ch])
-        copy = pltpu.make_async_copy(
-            stages[ch], placed.at[:, pl.ds(FPC * ch, FPC)], wsem.at[ch]
-        )
-        copy.start()
-        writes.append(copy)
-
-    writes = []
+        unpack_chunk(pos_s, recvs[ch], placed, FPC * ch)
+
     pack(0)
     pl.semaphore_wait(barrier, 127)
     send(0)
@@ -468,8 +470,6 @@
     pltpu.make_async_copy(marks.at[some], marks_in.at[some], msem.at[0]).wait()
     for ch in range(NCH):
         pltpu.make_async_copy(packs[ch].at[some], recvs[ch].at[some], ssem.at[ch]).wait()
-    for copy in writes:
-        copy.wait()
 
 
 SCRATCH = (
@@ -482,7 +482,6 @@
     [pltpu.VMEM((FPC, ROWS * 4, 128), F32)] * NCH,
     [pltpu.VMEM((ROWS, W, 128), F32)] * NCH,
     [pltpu.VMEM((ROWS, W, 128), F32)] * NCH,
-    [pltpu.VMEM((8, FPC, 64, 128), F32)] * NCH,
     pltpu.VMEM((16, 128), F32),
     pltpu.VMEM((128, 128), F32),
     pltpu.VMEM((128, 128), F32),
@@ -503,7 +502,6 @@
     pltpu.SemaphoreType.DMA((8,)),
     pltpu.SemaphoreType.DMA((8,)),
     pltpu.SemaphoreType.DMA((NCH,)),
-    pltpu.SemaphoreType.DMA((NCH,)),
     pltpu.SemaphoreType.DMA((NCH + 1,)),
     pltpu.SemaphoreType.DMA((2,)),
 )
@@ -517,10 +515,10 @@
     placed, correction = pl.pallas_call(
         whole_kernel,
         in_specs=[vmem, far] + [vmem] * 6,
-        out_specs=[far, vmem],
+        out_specs=[vmem, vmem],
         out_shape=[
-            jax.ShapeDtypeStruct((8, FIELDS, 64, 128), F32),
-            jax.ShapeDtypeStruct((512, 128), F32),
+            pltpu.VMEM((8, FIELDS, 64, 128), F32),
+            pltpu.VMEM((512, 128), F32),
         ],
         scratch_shapes=[SCRATCH],
         compiler_params=pltpu.CompilerParams(collective_id=1, has_side_effects=True),

time: 93.1 us -> 88.8 us (0.954)
  local copies, waits for them, and re-layouts: 4.88 us -> 2.37 us
  Pallas kernels: 87.4 us -> 85.7 us
    unnamed x4 -> x2, local copies, waits for them, and re-layouts: 4.88 us -> 2.37 us
    pallas_call x1, Pallas kernels: 87.4 us -> 85.7 us  [shards(): pl.pallas_call(whole_kernel, in_specs=[vmem, far] + [vmem] * 6, out_specs...]
where the time goes in v2:
time: 88.8 us; the launch traced here: 88.7 us
  Pallas kernels  85.7 us (97%)
  local copies, waits for them, and re-layouts  2.37 us (3%)
    pallas_call x1, Pallas kernels, shards(): pl.pallas_call(whole_kernel, in_specs=[vmem, far] + [vmem] * 6, out_specs...  85.7 us
    unnamed x2, local copies, waits for them, and re-layouts  2.37 us

profile of v2, /device:TPU:1, one launch (start us, length us, event | category | flops | bytes accessed | tf_op | source)
XLA Modules:
  0.0 88.7 jit_solution(14162599705893816646)
XLA Ops:
  0.6 85.7 %migrate_and_sweep.1 = (f32[8,12,64,128]{3,2,1,0:T(8,128)S(1)}, f32[512,128]{1,0:T(8,128)S(1)}) custom-call(s32[1,256]{1,0:T(1,128)} %bitcast.21, f32[12,1024,128]{2,1,0:T(8,128)} %bitcast.19, f32[10,10]{1,0:T(8,128)} %vx.1, f32[10,10]{1,0:T(8,128)} %vs.1, f32[10,16,10]{2,1,0:T(8,128)} %bitcast.20, f32[1,10]{1,0:T(1,128)} %bitcast.22, f32[1,10]{1,0:T(1,128)} %bitcast.23, ...), custom_call_target="tpu_custom_call" | custom-call | tf_op jit(solution)/shard_map/migrate_and_sweep/pallas_call | solution.py:515
  86.3 1.7 %copy.12 = f32[4,2,16,12,512]{4,2,3,1,0:T(8,128)} copy(f32[4,2,16,12,512]{4,2,3,1,0:T(8,128)S(1)} %bitcast.17) | data formatting | bytes 6291456
  88.0 0.7 copy.13

commit v3 on v2

--- a/solution.py
+++ b/solution.py
@@ -14,6 +14,7 @@
 FPC = 2
 NCH = FIELDS // FPC
 W = 4 * FPC
+VMEM_LIMIT = 61_000_000
 ROWS = 256
 
 
@@ -133,16 +134,23 @@
 
 
 def right_side(arrived, marks, points):
-    nf = lane_iota(ROWS).astype(F32)
-    chosen = jnp.where(marks == nf, 1.0, 0.0)
+    nf = lane_iota(128).astype(F32)
+    chosen = [jnp.where(mark == nf, 1.0, 0.0) for mark in split_marks(marks)]
     for c in range(4):
-        f0, f1, f2 = (
-            arrived[f // FPC][pl.ds(4 * (f % FPC) + c, ROWS, stride=W), :] for f in range(3)
-        )
-        rows = 3.0 * f0 - 3.0 * f1 + f2
-        points[128 * c : 128 * (c + 1), :] = jnp.dot(
-            rows.T, chosen, precision=HIGHEST, preferred_element_type=F32
-        )
+        total = None
+        for slot in range(2):
+            f0, f1, f2 = (
+                arrived[f // FPC][
+                    pl.ds(slot * W + 4 * (f % FPC) + c, 128, stride=2 * W), :
+                ]
+                for f in range(3)
+            )
+            rows = 3.0 * f0 - 3.0 * f1 + f2
+            part = jnp.dot(
+                rows.T, chosen[slot], precision=HIGHEST, preferred_element_type=F32
+            )
+            total = part if total is None else total + part
+        points[128 * c : 128 * (c + 1), :] = total
 
 
 def gather_planes(points, planes):
@@ -161,11 +169,43 @@
     )
 
 
-def plane_copies(sources, target, ssem, rsem, base):
+def squeeze_plane(p, read, wire):
+    lane = lane_iota(16)
+    if p < 2:
+        first = 96 if p == 0 else 0
+        total = None
+        for q in range(4):
+            turn = (32 * q - first) % 128
+            rows = read(16 * q, 16)
+            rows = pltpu.roll(rows, turn, 1) if turn else rows
+            total = rows if q == 0 else jnp.where((lane >> 5) == q, rows, total)
+        wire[...] = total
+    else:
+        upper = (lane & 16) != 0
+        for half in range(2):
+            near, moved = read(16 * half, 16), read(32 + 16 * half, 16)
+            moved = pltpu.roll(moved, 112 if p == 2 else 16, 1)
+            keep = upper if p == 2 else ~upper
+            wire[16 * half : 16 * half + 16, :] = jnp.where(keep, near, moved)
+
+
+def widen_plane(p, wire, plane):
+    if p < 2:
+        first = 96 if p == 0 else 0
+        for q in range(4):
+            turn = (first - 32 * q) % 128
+            rows = pltpu.roll(wire[...], turn, 1) if turn else wire[...]
+            plane[p, 16 * q : 16 * q + 16, :] = rows
+    else:
+        plane[p, 0:32, :] = wire[...]
+        plane[p, 32:64, :] = pltpu.roll(wire[...], 16 if p == 2 else 112, 1)
+
+
+def plane_copies(sources, targets, ssem, rsem, base):
     return [
         pltpu.make_async_remote_copy(
             sources[p],
-            target.at[p],
+            targets[p],
             ssem.at[base + p],
             rsem.at[base + p],
             device_id=peer,
@@ -308,9 +348,13 @@
     pos_c = jnp.sum(jnp.where(same, pos_b, 0.0), axis=1, keepdims=True)
     idx = jnp.sum(jnp.where(pos_c == cf, rf, 0.0), axis=0, keepdims=True)
     idx_v[...] = idx.astype(jnp.int32)
-    row_b = jnp.broadcast_to(row + 1.0, (ROWS, ROWS))
-    mark = jnp.sum(jnp.where(pos_b == rf, row_b, 0.0), axis=1, keepdims=True) - 1.0
-    marks[...] = jnp.broadcast_to(mark, (ROWS, 128)).reshape(ROWS, 1, 128)
+    row_b = jnp.broadcast_to(row + 1.0, (128, ROWS))
+    pos_b = jnp.broadcast_to(pos, (128, ROWS))
+    even = lax.broadcasted_iota(jnp.int32, (128, ROWS), 0).astype(F32) * 2.0
+    mark0 = jnp.sum(jnp.where(pos_b == even, row_b, 0.0), axis=1, keepdims=True) - 1.0
+    mark1 = jnp.sum(jnp.where(pos_b == even + 1.0, row_b, 0.0), axis=1, keepdims=True) - 1.0
+    both = jnp.where(lane_iota(128) < 64, mark0, mark1)
+    marks[...] = both.reshape(128, 1, 128)
 
 
 def pack_chunk(idx_s, old, packed):
@@ -326,10 +370,19 @@
     lax.fori_loop(0, ROWS // 4, body, 0)
 
 
+def split_marks(marks):
+    return (
+        jnp.broadcast_to(marks[:, 0:1], (128, 128)),
+        jnp.broadcast_to(marks[:, 64:65], (128, 128)),
+    )
+
+
 def arrived_rows(marks, idx_v):
-    rf = lax.broadcasted_iota(jnp.int32, (ROWS, 128), 0).astype(F32)
-    nf = lane_iota(ROWS).astype(F32)
-    idx = jnp.sum(jnp.where(marks == nf, rf, 0.0), axis=0, keepdims=True)
+    even = lax.broadcasted_iota(jnp.int32, (128, 128), 0).astype(F32) * 2.0
+    mark0, mark1 = split_marks(marks)
+    nf = lane_iota(128).astype(F32)
+    idx = jnp.where(mark0 == nf, even, 0.0) + jnp.where(mark1 == nf, even + 1.0, 0.0)
+    idx = jnp.sum(idx, axis=0, keepdims=True)
     idx_v[...] = idx.astype(jnp.int32)
 
 
@@ -347,12 +400,13 @@
     lax.fori_loop(0, 8, body, 0)
 
 
-def whole_kernel(place, old, vx, vs, vw, valx, vals, valw, placed, out, scratch):
+def whole_kernel(place, old, vx, vs, vw, valx, vals, valw, placed, out, tail, pos_v, scratch):
     (
-        idx_v, idx_s, pos_v, pos_s, marks, marks_in, olds, packs, recvs,
+        idx_v, idx_s, pos_s, marks, marks_in, olds, packs, recvs,
         pad, mat, mat_t, coef, wval, dcol, points, faces, faces_in, boxes, half,
-        planes, planes_in, sums, ssem, rsem, msem, hssem, hrsem, osem, lsem, isem,
+        planes, planes_in, sums, wires, ssem, rsem, msem, hssem, hrsem, osem, lsem, isem,
     ) = scratch
+    recvs = list(recvs) + [tail]
     gx, gy = my_place()
     me = gx * 8 + gy
     everyone = peers(ORDER)
@@ -363,17 +417,11 @@
         pltpu.make_async_copy(old.at[pl.ds(FPC * ch, FPC)], olds[ch], osem.at[ch])
         for ch in range(NCH)
     ]
+
+    for peer in last:
+        pl.semaphore_signal(barrier, inc=1, device_id=peer, device_id_type=MESH)
     for copy in loads:
         copy.start()
-
-    def greet(k, _):
-        d = lax.rem(me + k, 128)
-        pl.semaphore_signal(
-            barrier, inc=1, device_id=(d // 8, lax.rem(d, 8)), device_id_type=MESH
-        )
-        return 0
-
-    lax.fori_loop(1, 128, greet, 0)
     target_rows(place[...], idx_v, marks)
     copy = pltpu.make_async_copy(idx_v, idx_s, isem.at[0])
     copy.start()
@@ -395,6 +443,16 @@
             device_id_type=MESH,
         ).start()
 
+    def send_marks(peer):
+        pltpu.make_async_remote_copy(
+            marks.at[pl.ds(peer[0] * 8 + peer[1], 1)],
+            marks_in.at[pl.ds(me, 1)],
+            msem.at[0],
+            msem.at[1],
+            device_id=peer,
+            device_id_type=MESH,
+        ).start()
+
     def keep_own(source, target, sem):
         copy = pltpu.make_async_copy(
             source.at[pl.ds(2 * me, 2)], target.at[pl.ds(2 * me, 2)], sem
@@ -420,19 +478,21 @@
     pl.semaphore_wait(barrier, 127)
     send(0)
     for peer in everyone:
-        send_one(marks, marks_in, msem.at[0], msem.at[1], peer)
+        send_marks(peer)
     pack(1)
     send(1)
-    keep_own(marks, marks_in, lsem.at[NCH])
+    own_marks = pltpu.make_async_copy(
+        marks.at[pl.ds(me, 1)], marks_in.at[pl.ds(me, 1)], lsem.at[NCH]
+    )
+    own_marks.start()
     pack(2)
-    own_marks = own.pop()
     send(2)
     for ch in range(3, NCH):
         pack(ch)
     build_tables(vx, vs, vw, valx, vals, valw, pad, mat, mat_t, coef, wval, dcol)
-    pltpu.make_async_copy(marks.at[some], marks_in.at[some], msem.at[1]).wait()
+    pltpu.make_async_copy(marks.at[pl.ds(0, 127)], marks_in.at[pl.ds(0, 127)], msem.at[1]).wait()
     own_marks.wait()
-    marks_here = marks_in[...].reshape(ROWS, 128)
+    marks_here = marks_in[...].reshape(128, 128)
     arrived_rows(marks_here, pos_v)
     copy = pltpu.make_async_copy(pos_v, pos_s, isem.at[1])
     copy.start()
@@ -441,47 +501,80 @@
     arrive(1)
     right_side([recvs[ch].reshape(ROWS * W, 128) for ch in range(2)], marks_here, points)
     gather_planes(points, faces)
-    sources = (points.at[pl.ds(448, 64)], points.at[pl.ds(0, 64)], faces.at[0], faces.at[1])
-    halo = plane_copies(sources, faces_in, hssem, hrsem, 0)
+    reads = (
+        lambda at, n: points[448 + at : 448 + at + n, :],
+        lambda at, n: points[at : at + n, :],
+        lambda at, n: faces[0, at : at + n, :],
+        lambda at, n: faces[1, at : at + n, :],
+    )
+    for p in range(4):
+        squeeze_plane(p, reads[p], wires[p])
+    halo = plane_copies(wires[0:4], wires[4:8], hssem, hrsem, 0)
     for copy in halo:
         copy.start()
     send(3)
     fill_inner(points, boxes)
     unpack(0)
     unpack(1)
-    for copy in halo:
+    for p, copy in enumerate(halo):
         copy.wait()
+        widen_plane(p, wires[4 + p], faces_in)
     fill_faces(points, faces, faces_in, boxes)
     solve_boxes(boxes, half, mat, mat_t, coef, wval, dcol)
     return_planes(boxes, planes)
-    halo = plane_copies([planes.at[p] for p in range(4)], planes_in, hssem, hrsem, 4)
+    for p in range(4):
+        squeeze_plane(p, lambda at, n, p=p: planes[p, at : at + n, :], wires[8 + p])
+    halo = plane_copies(wires[8:12], wires[12:16], hssem, hrsem, 4)
     for copy in halo:
         copy.start()
     send(4)
     send(5)
     arrive(2)
     unpack(2)
-    for copy in halo:
+    for p, copy in enumerate(halo):
         copy.wait()
+        widen_plane(p, wires[12 + p], planes_in)
     sum_cells(planes, planes_in, boxes, sums, out)
-    for ch in range(3, NCH):
+    for ch in range(3, NCH - 1):
         arrive(ch)
         unpack(ch)
-    pltpu.make_async_copy(marks.at[some], marks_in.at[some], msem.at[0]).wait()
+    arrive(NCH - 1)
+    pltpu.make_async_copy(marks.at[pl.ds(0, 127)], marks_in.at[pl.ds(0, 127)], msem.at[0]).wait()
     for ch in range(NCH):
         pltpu.make_async_copy(packs[ch].at[some], recvs[ch].at[some], ssem.at[ch]).wait()
+
+
+def publish_kernel(placed, correction, tail, pos_v, new_states, out, stage, pos_s, sems):
+    index = pltpu.make_async_copy(pos_v, pos_s, sems.at[17])
+    index.start()
+    done = FIELDS - FPC
+    copies = [
+        pltpu.make_async_copy(placed.at[c], new_states.at[c, pl.ds(0, done)], sems.at[c])
+        for c in range(8)
+    ]
+    copies.append(pltpu.make_async_copy(correction, out, sems.at[16]))
+    for copy in copies:
+        copy.start()
+    index.wait()
+    unpack_chunk(pos_s, tail, stage, 0)
+    for c in range(8):
+        copies.append(
+            pltpu.make_async_copy(stage.at[c], new_states.at[c, pl.ds(done, FPC)], sems.at[8 + c])
+        )
+        copies[-1].start()
+    for copy in copies:
+        copy.wait()
 
 
 SCRATCH = (
     pltpu.VMEM((1, ROWS), jnp.int32),
     pltpu.SMEM((1, ROWS), jnp.int32),
-    pltpu.VMEM((1, 128), jnp.int32),
     pltpu.SMEM((1, 128), jnp.int32),
-    pltpu.VMEM((ROWS, 1, 128), F32),
-    pltpu.VMEM((ROWS, 1, 128), F32),
+    pltpu.VMEM((128, 1, 128), F32),
+    pltpu.VMEM((128, 1, 128), F32),
     [pltpu.VMEM((FPC, ROWS * 4, 128), F32)] * NCH,
     [pltpu.VMEM((ROWS, W, 128), F32)] * NCH,
-    [pltpu.VMEM((ROWS, W, 128), F32)] * NCH,
+    [pltpu.VMEM((ROWS, W, 128), F32)] * (NCH - 1),
     pltpu.VMEM((16, 128), F32),
     pltpu.VMEM((128, 128), F32),
     pltpu.VMEM((128, 128), F32),
@@ -496,6 +589,7 @@
     pltpu.VMEM((4, 64, 128), F32),
     pltpu.VMEM((4, 64, 128), F32),
     pltpu.VMEM((8, 64, 128), F32),
+    [pltpu.VMEM((rows, 128), F32) for rows in (16, 16, 32, 32) * 4],
     pltpu.SemaphoreType.DMA((NCH,)),
     pltpu.SemaphoreType.DMA((NCH,)),
     pltpu.SemaphoreType.DMA((2,)),
@@ -512,16 +606,20 @@
     old_view = old_view.transpose(0, 1, 3, 2, 4).reshape(FIELDS, ROWS * 4, 128)
     vmem = pl.BlockSpec(memory_space=pltpu.VMEM)
     far = pl.BlockSpec(memory_space=pl.ANY)
-    placed, correction = pl.pallas_call(
+    results = pl.pallas_call(
         whole_kernel,
         in_specs=[vmem, far] + [vmem] * 6,
-        out_specs=[vmem, vmem],
+        out_specs=[vmem] * 4,
         out_shape=[
-            pltpu.VMEM((8, FIELDS, 64, 128), F32),
+            pltpu.VMEM((8, FIELDS - FPC, 64, 128), F32),
             pltpu.VMEM((512, 128), F32),
+            pltpu.VMEM((ROWS, W, 128), F32),
+            pltpu.VMEM((1, 128), jnp.int32),
         ],
         scratch_shapes=[SCRATCH],
-        compiler_params=pltpu.CompilerParams(collective_id=1, has_side_effects=True),
+        compiler_params=pltpu.CompilerParams(
+            collective_id=1, has_side_effects=True, vmem_limit_bytes=VMEM_LIMIT
+        ),
         name="migrate_and_sweep",
     )(
         new_place.reshape(1, ROWS),
@@ -533,6 +631,22 @@
         values_s.reshape(1, 10),
         values_w,
     )
+    placed, correction = pl.pallas_call(
+        publish_kernel,
+        in_specs=[vmem] * 4,
+        out_specs=[far] * 2,
+        out_shape=[
+            jax.ShapeDtypeStruct((8, FIELDS, 64, 128), F32),
+            jax.ShapeDtypeStruct((512, 128), F32),
+        ],
+        scratch_shapes=[
+            pltpu.VMEM((8, FPC, 64, 128), F32),
+            pltpu.SMEM((1, 128), jnp.int32),
+            pltpu.SemaphoreType.DMA((18,)),
+        ],
+        compiler_params=pltpu.CompilerParams(vmem_limit_bytes=VMEM_LIMIT),
+        name="publish",
+    )(*(pltpu.with_memory_space_constraint(r, pltpu.VMEM) for r in results))
     placed = placed.reshape(4, 2, FIELDS, 2, 4, 8, 128).transpose(0, 1, 3, 5, 2, 4, 6)
     return placed.reshape(4, 2, 16, FIELDS, 512), correction.reshape(32, 16, 128)
 

time: 88.8 us -> 85.1 us (0.958)
  local copies, waits for them, and re-layouts: 2.37 us -> 0 us
  Pallas kernels: 85.7 us -> 84.3 us
    pallas_call x1, Pallas kernels: 85.7 us -> 82.4 us  [shards(): pl.pallas_call(whole_kernel, in_specs=[vmem, far] + [vmem] * 6, out_specs...]
    unnamed x2 -> x0, local copies, waits for them, and re-layouts: 2.37 us -> none
    pallas_call x0 -> x1, Pallas kernels: none -> 1.89 us  [shards(): pl.pallas_call(publish_kernel, in_specs=[vmem] * 4, out_specs=[far] * 2,...]
where the time goes in v3:
time: 85.1 us; the launch traced here: 85 us
  Pallas kernels  84.3 us (99%)
    pallas_call x1, Pallas kernels, shards(): pl.pallas_call(whole_kernel, in_specs=[vmem, far] + [vmem] * 6, out_specs...  82.4 us
    pallas_call x1, Pallas kernels, shards(): pl.pallas_call(publish_kernel, in_specs=[vmem] * 4, out_specs=[far] * 2,...  1.89 us

profile of v3, /device:TPU:1, one launch (start us, length us, event | category | flops | bytes accessed | tf_op | source)
XLA Modules:
  0.0 85.0 jit_solution(6949965591746052977)
XLA Ops:
  0.6 82.4 %migrate_and_sweep.1 = (f32[8,10,64,128]{3,2,1,0:T(8,128)S(1)}, f32[512,128]{1,0:T(8,128)S(1)}, f32[256,8,128]{2,1,0:T(8,128)S(1)}, s32[1,128]{1,0:T(1,128)S(1)}) custom-call(s32[1,256]{1,0:T(1,128)} %bitcast.19, f32[12,1024,128]{2,1,0:T(8,128)} %bitcast.17, f32[10,10]{1,0:T(8,128)} %vx.1, f32[10,10]{1,0:T(8,128)} %vs.1, f32[10,16,10]{2,1,0:T(8,128)} %bitcast.18, ...), custom_call_target="tpu_custom_call" | custom-call | tf_op jit(solution)/shard_map/migrate_and_sweep/pallas_call | solution.py:609
  83.1 1.9 %publish.1 = (f32[8,12,64,128]{3,2,1,0:T(8,128)}, f32[512,128]{1,0:T(8,128)}) custom-call(f32[8,10,64,128]{3,2,1,0:T(8,128)S(1)} %get-tuple-element.8.placed, f32[512,128]{1,0:T(8,128)S(1)} %get-tuple-element.9.correction, f32[256,8,128]{2,1,0:T(8,128)S(1)} %get-tuple-element.10.tail, s32[1,128]{1,0:T(1,128)S(1)} %get-tuple-element.11.pos_v), custom_call_target="tpu_custom_call" | custom-call | tf_op jit(solution)/shard_map/publish/pallas_call | solution.py:634

commit v4 on v3

--- a/solution.py
+++ b/solution.py
@@ -400,13 +400,20 @@
     lax.fori_loop(0, 8, body, 0)
 
 
-def whole_kernel(place, old, vx, vs, vw, valx, vals, valw, placed, out, tail, pos_v, scratch):
+def whole_kernel(place_far, old, vx, vs, vw, valx, vals, valw, placed, out, tail, pos_v, scratch):
     (
         idx_v, idx_s, pos_s, marks, marks_in, olds, packs, recvs,
         pad, mat, mat_t, coef, wval, dcol, points, faces, faces_in, boxes, half,
-        planes, planes_in, sums, wires, ssem, rsem, msem, hssem, hrsem, osem, lsem, isem,
+        planes, planes_in, sums, wires, smalls, tsem, ssem, rsem, msem, hssem, hrsem, osem, lsem, isem,
     ) = scratch
     recvs = list(recvs) + [tail]
+    place, *tables = smalls
+    place_load = pltpu.make_async_copy(place_far, place, tsem.at[6])
+    place_load.start()
+    table_loads = [
+        pltpu.make_async_copy(value, table, tsem.at[i])
+        for i, (value, table) in enumerate(zip((vx, vs, vw, valx, vals, valw), tables))
+    ]
     gx, gy = my_place()
     me = gx * 8 + gy
     everyone = peers(ORDER)
@@ -420,8 +427,9 @@
 
     for peer in last:
         pl.semaphore_signal(barrier, inc=1, device_id=peer, device_id_type=MESH)
-    for copy in loads:
+    for copy in loads + table_loads:
         copy.start()
+    place_load.wait()
     target_rows(place[...], idx_v, marks)
     copy = pltpu.make_async_copy(idx_v, idx_s, isem.at[0])
     copy.start()
@@ -489,7 +497,9 @@
     send(2)
     for ch in range(3, NCH):
         pack(ch)
-    build_tables(vx, vs, vw, valx, vals, valw, pad, mat, mat_t, coef, wval, dcol)
+    for copy in table_loads:
+        copy.wait()
+    build_tables(*tables, pad, mat, mat_t, coef, wval, dcol)
     pltpu.make_async_copy(marks.at[pl.ds(0, 127)], marks_in.at[pl.ds(0, 127)], msem.at[1]).wait()
     own_marks.wait()
     marks_here = marks_in[...].reshape(128, 128)
@@ -590,6 +600,9 @@
     pltpu.VMEM((4, 64, 128), F32),
     pltpu.VMEM((8, 64, 128), F32),
     [pltpu.VMEM((rows, 128), F32) for rows in (16, 16, 32, 32) * 4],
+    [pltpu.VMEM((1, ROWS), jnp.int32)]
+    + [pltpu.VMEM(s, F32) for s in ((10, 10), (10, 10), (10, 16, 10), (1, 10), (1, 10), (16, 10))],
+    pltpu.SemaphoreType.DMA((7,)),
     pltpu.SemaphoreType.DMA((NCH,)),
     pltpu.SemaphoreType.DMA((NCH,)),
     pltpu.SemaphoreType.DMA((2,)),
@@ -608,7 +621,7 @@
     far = pl.BlockSpec(memory_space=pl.ANY)
     results = pl.pallas_call(
         whole_kernel,
-        in_specs=[vmem, far] + [vmem] * 6,
+        in_specs=[far] * 8,
         out_specs=[vmem] * 4,
         out_shape=[
             pltpu.VMEM((8, FIELDS - FPC, 64, 128), F32),

time: 85.1 us -> 84.4 us (level)
  no operation moved by 1% of the time
where the time goes in v4:
time: 84.4 us; the launch traced here: 84.3 us
  Pallas kernels  83.7 us (99%)
    pallas_call x1, Pallas kernels, shards(): pl.pallas_call(whole_kernel, in_specs=[far] * 8, out_specs=[vmem] * 4, ou...  81.8 us
    pallas_call x1, Pallas kernels, shards(): pl.pallas_call(publish_kernel, in_specs=[vmem] * 4, out_specs=[far] * 2,...  1.89 us

profile of v4, /device:TPU:1, one launch (start us, length us, event | category | flops | bytes accessed | tf_op | source)
XLA Modules:
  0.0 84.3 jit_solution(8387345305096504990)
XLA Ops:
  0.6 81.8 %migrate_and_sweep.1 = (f32[8,10,64,128]{3,2,1,0:T(8,128)S(1)}, f32[512,128]{1,0:T(8,128)S(1)}, f32[256,8,128]{2,1,0:T(8,128)S(1)}, s32[1,128]{1,0:T(1,128)S(1)}) custom-call(s32[1,256]{1,0:T(1,128)} %bitcast.19, f32[12,1024,128]{2,1,0:T(8,128)} %bitcast.17, f32[10,10]{1,0:T(8,128)} %vx.1, f32[10,10]{1,0:T(8,128)} %vs.1, f32[10,16,10]{2,1,0:T(8,128)} %bitcast.18, ...), custom_call_target="tpu_custom_call" | custom-call | tf_op jit(solution)/shard_map/migrate_and_sweep/pallas_call | solution.py:622
  82.4 1.9 %publish.1 = (f32[8,12,64,128]{3,2,1,0:T(8,128)}, f32[512,128]{1,0:T(8,128)}) custom-call(f32[8,10,64,128]{3,2,1,0:T(8,128)S(1)} %get-tuple-element.8.placed, f32[512,128]{1,0:T(8,128)S(1)} %get-tuple-element.9.correction, f32[256,8,128]{2,1,0:T(8,128)S(1)} %get-tuple-element.10.tail, s32[1,128]{1,0:T(1,128)S(1)} %get-tuple-element.11.pos_v), custom_call_target="tpu_custom_call" | custom-call | tf_op jit(solution)/shard_map/publish/pallas_call | solution.py:647

commit v5 on v4

--- a/solution.py
+++ b/solution.py
@@ -63,16 +63,18 @@
     y, core = gy // 2, lax.rem(gy, 2)
     other = 1 - core
     out = [(gx, y * 2 + other)]
-    pairs = [(to, step) for to in (core, other) for step in steps]
+    pairs = [(to, step) for to in (0, 1) for step in steps]
     if steps is LAST:
-        pairs = [(to, step) for step in steps for to in (core, other)]
-    for to_core, step in pairs:
-        if True:
-            hop = [step[i] * (1 - core) + (4 - step[i]) * core for i in range(3)]
-            px = lax.rem(x + hop[0], 4)
-            py = lax.rem(y + hop[1], 4)
-            pz = lax.rem(z + hop[2], 4)
-            out.append((px * 4 + pz, py * 2 + to_core))
+        pairs = [(to, step) for step in steps for to in (0, 1)]
+    hops = [lax.rem(4 + d - 2 * d * core, 4) for d in range(4)]
+    hops[2] = 2
+    xs = [lax.rem(x + hop, 4) * 4 for hop in hops]
+    zs = [lax.rem(z + hop, 4) for hop in hops]
+    gxs = [[px + pz for pz in zs] for px in xs]
+    ys = [lax.rem(y + hop, 4) * 2 for hop in hops]
+    gys = [(py + core, py + other) for py in ys]
+    for to, step in pairs:
+        out.append((gxs[step[0]][step[2]], gys[step[1]][to]))
     return out
 
 

time: 84.4 us -> 84.4 us (level)
  no operation moved by 1% of the time
where the time goes in v5:
time: 84.4 us; the launch traced here: 84.3 us
  Pallas kernels  83.6 us (99%)
    pallas_call x1, Pallas kernels, shards(): pl.pallas_call(whole_kernel, in_specs=[far] * 8, out_specs=[vmem] * 4, ou...  81.8 us
    pallas_call x1, Pallas kernels, shards(): pl.pallas_call(publish_kernel, in_specs=[vmem] * 4, out_specs=[far] * 2,...  1.89 us

profile of v5, /device:TPU:1, one launch (start us, length us, event | category | flops | bytes accessed | tf_op | source)
XLA Modules:
  0.0 84.3 jit_solution(15731185976988752431)
XLA Ops:
  0.6 81.8 %migrate_and_sweep.1 = (f32[8,10,64,128]{3,2,1,0:T(8,128)S(1)}, f32[512,128]{1,0:T(8,128)S(1)}, f32[256,8,128]{2,1,0:T(8,128)S(1)}, s32[1,128]{1,0:T(1,128)S(1)}) custom-call(s32[1,256]{1,0:T(1,128)} %bitcast.19, f32[12,1024,128]{2,1,0:T(8,128)} %bitcast.17, f32[10,10]{1,0:T(8,128)} %vx.1, f32[10,10]{1,0:T(8,128)} %vs.1, f32[10,16,10]{2,1,0:T(8,128)} %bitcast.18, ...), custom_call_target="tpu_custom_call" | custom-call | tf_op jit(solution)/shard_map/migrate_and_sweep/pallas_call | solution.py:624
  82.4 1.9 %publish.1 = (f32[8,12,64,128]{3,2,1,0:T(8,128)}, f32[512,128]{1,0:T(8,128)}) custom-call(f32[8,10,64,128]{3,2,1,0:T(8,128)S(1)} %get-tuple-element.8.placed, f32[512,128]{1,0:T(8,128)S(1)} %get-tuple-element.9.correction, f32[256,8,128]{2,1,0:T(8,128)S(1)} %get-tuple-element.10.tail, s32[1,128]{1,0:T(1,128)S(1)} %get-tuple-element.11.pos_v), custom_call_target="tpu_custom_call" | custom-call | tf_op jit(solution)/shard_map/publish/pallas_call | solution.py:649
